TPU v7x, 256 devices: a whole 4x4x8 slice. The times are simulated.
256 devices in a mesh: frame: 8 (over z_lo, x), brick: 32 (over y, z_hi, core).
Axes of the slice: x: 4, y: 4, z: 8 (z_hi: 4, z_lo: 2; z = z_hi * 2 + z_lo), core: 2. Of those that a mesh axis runs over, the one named last changes fastest.
Arguments:
- intensity: float32 [32, 512, 128], P('frame', 'brick'), may hold values from 0.1 to 10
- correction: float32 [32, 512, 128], P('frame', 'brick'), may hold values from 0.3 to 3
- splitting: bfloat16 [32, 32, 8, 128, 512], P('frame', 'brick'), may hold values from 0 to 0.015625
- block_count: int32 [32, 32], P('frame', 'brick'), may hold values from 1 to 8, 128 in all within a row
- pix_index: int32 [32, 32, 8], P('frame', 'brick'), may hold values from 0 to 511, as said below
- vox_offset: int32 [32, 32, 8], P('frame', 'brick'), may hold values from 0 to 129
Outputs:
- merged: float32 [32, 128, 512], P('brick', 'frame')
- weight: float32 [32, 128, 512], P('brick', 'frame')
Inputs may be any that keep to these rules, and one draw needn't show every extreme that they name: `block_count`: each frame's counts over the bricks sum to 128, and some pair of the frame holds 8. `pix_index`: the 32 slots of one device (its frames, its brick, padded slots included) include at most 4 slots (counted with repeats, over all of the device's frames) whose pixel block lies in the range 16 * c to 16 * c + 15, for every c; on every device some c has exactly 4 such slots.
All inputs are finite; a program needn't handle non-finite values. No bound on the sum of `block_count` on one device may be relied on, other than what follows from the above.
Results may differ from a plain program's by a relative error of at most 0.00049.
Values may be sent and summed in bfloat16 or wider, within the bound.
A program may use at most 64 MiB of HBM per device.

v0:
```python
import jax
import jax.numpy as jnp
from jax import lax
from jax.sharding import PartitionSpec as P

BLK_DEV = 16


def extended(block, sides, width):
    for axis, dim in sides:
        count = lax.axis_size(axis)
        forward = [(i, i + 1) for i in range(count - 1)]
        backward = [(target, source) for source, target in forward]
        low = lax.ppermute(
            lax.slice_in_dim(block, block.shape[dim] - width, None, axis=dim), axis, forward
        )
        high = lax.ppermute(lax.slice_in_dim(block, 0, width, axis=dim), axis, backward)
        block = jnp.concatenate([low, block, high], axis=dim)
    return block


def on_device(intensity, correction, splitting, block_count, pix_index, vox_offset):
    frames_dev, blocks_per_device, pixel_width = intensity.shape
    max_slots = splitting.shape[2]
    voxels = splitting.shape[4]
    bricks = lax.axis_size("brick")
    groups = lax.axis_size("frame")
    block_rows = BLK_DEV * groups
    slot_count = frames_dev * max_slots
    local_rows = jnp.stack([intensity, correction], axis=2).astype(jnp.bfloat16)
    indices = pix_index.reshape(slot_count)
    frame_slot = jnp.arange(slot_count, dtype=jnp.int32) // max_slots
    gathered = lax.all_gather(local_rows, "brick", axis=1, tiled=True)
    flat_rows = gathered.reshape(frames_dev * blocks_per_device * bricks, 2, pixel_width)
    rows_per_slot = flat_rows[frame_slot * (blocks_per_device * bricks) + indices]
    divided_blocks = splitting.reshape(slot_count, pixel_width, voxels)
    contrib = jnp.einsum(
        "edb,eba->eda", rows_per_slot, divided_blocks, preferred_element_type=jnp.float32
    )
    flat_contrib = contrib.reshape(slot_count, 2 * voxels)
    live_slots = (jnp.arange(max_slots, dtype=jnp.int32)[None, :] < block_count).reshape(slot_count)
    offsets = vox_offset.reshape(slot_count)
    edge_ids = jnp.array([0, block_rows + 1], dtype=jnp.int32)[:, None]
    edge_place = ((offsets[None, :] == edge_ids) & live_slots[None, :]).astype(jnp.float32)
    overhang = jnp.dot(
        edge_place,
        flat_contrib,
        precision=lax.Precision.HIGHEST,
        preferred_element_type=jnp.float32,
    ).reshape(2, 2, voxels)
    neighbours = extended(overhang, (("brick", 0),), 1)
    lower_add = neighbours[0]
    upper_increment = neighbours[3]
    row_ids = jnp.arange(1, block_rows + 1, dtype=jnp.int32)[:, None]
    placement = ((offsets[None, :] == row_ids) & live_slots[None, :]).astype(jnp.float32)
    interior = jnp.dot(
        placement, flat_contrib, precision=lax.Precision.HIGHEST, preferred_element_type=jnp.float32
    )
    interior = interior.reshape(block_rows, 2, voxels)
    interior = interior.at[0].add(lower_add).at[block_rows - 1].add(upper_increment)
    reduced = lax.psum_scatter(interior, "frame", scatter_dimension=0, tiled=True)
    weight = reduced[:, 1]
    merged = reduced[:, 0] / jnp.maximum(weight, 1.0)
    return (merged[None], weight[None])


def solution(mesh):
    placed = (
        P("frame", "brick", None),
        P("frame", "brick", None),
        P("frame", "brick", None, None, None),
        P("frame", "brick"),
        P("frame", "brick", None),
        P("frame", "brick", None),
    )
    return jax.shard_map(
        on_device,
        mesh=mesh,
        in_specs=placed,
        out_specs=(P("brick", "frame", None), P("brick", "frame", None)),
        check_vma=False,
    )
```

profile of v0, /device:TPU:8, one launch (start us, length us, event | category | flops | bytes accessed | tf_op | source)
XLA Modules:
  0.0 130.7 jit_solution(8027460333084453383)
XLA Ops:
  7.2 0.0 all-gather.2.cloned.1.call-start
  7.2 0.8 convert_bitcast_fusion
  8.0 0.6 pad_maximum_fusion
  8.6 0.0 all-gather.2.cloned.1.call-update
  8.6 0.0 reduce-scatter.2.cloned.1.call-start
  8.7 0.5 broadcast.132
  9.2 1.3 %reduce.10 = s32[4,8]{1,0:T(4,128)S(1)} reduce(s32[4,1,8]{2,1,0:T(1,128)} %param.15, s32[]{:T(128)} %broadcast.132), dimensions={1}, to_apply=%param.15.reduce_sub_computation.3 | reduce | bytes 260 | tf_op args[4]
  10.5 0.1 reshape.176
  10.6 1.3 %reduce.11 = s32[4,8]{1,0:T(4,128)S(1)} reduce(s32[4,1,8]{2,1,0:T(1,128)} %param.16, s32[]{:T(128)} %broadcast.132), dimensions={1}, to_apply=%param.16.reduce_sub_computation.3 | reduce | bytes 260 | tf_op args[5]
  12.0 0.1 eq.28
  12.1 0.7 iota_compare_fusion
  12.8 0.1 lt.37
  12.9 51.9 %all-gather.2.cloned.1.call-done = bf16[4,512,2,128]{3,1,0,2:T(8,128)(2,1)} async-done(((bf16[4,16,2,128]{3,1,0,2:T(8,128)(2,1)}), bf16[4,512,2,128]{3,1,0,2:T(8,128)(2,1)}) %all-gather.2.cloned.1.call-update) | async-done | bytes 1048592 | tf_op jit(solution)/shard_map/all_gather | solution.py:33
  64.8 2.3 %copy.9 = bf16[4,512,2,128]{3,2,1,0:T(2,128)(2,1)S(1)} copy(bf16[4,512,2,128]{3,1,0,2:T(8,128)(2,1)} %all-gather.2.cloned.1.call-done) | data formatting | bytes 2097152 | tf_op jit(solution)/shard_map/all_gather | solution.py:33
  67.1 0.6 gather_fusion
  67.7 2.8 %fusion.20 = f32[32,2,512]{2,1,0:T(2,128)S(1)} fusion(bf16[32,2,128]{2,1,0:T(2,128)(2,1)S(1)} %gather_fusion, bf16[32,128,512]{2,1,0:T(8,128)(2,1)} %bitcast.35), kind=kOutput, calls=%fused_computation.38 | convolution fusion | flops 8388608 | bytes 4341760 | tf_op jit(solution)/shard_map/edb,eba->eda/dot_general | solution.py:37
  70.6 0.2 fusion.10
  70.8 2.1 %collective-permute-start = (f32[1,2,512]{2,0,1:T(1,128)S(1)}, f32[1,2,512]{2,0,1:T(1,128)S(1)}, u32[]{:S(2)}, u32[]{:S(2)}) collective-permute-start(f32[1,2,512]{2,0,1:T(1,128)S(1)} %bitcast.41), channel_id=1, source_target_pairs={{0,1},{1,2},{2,3},{3,4},{4,5},{5,6},{6,7},{7,8},{8,9},{9,10},{10,1... | collective-permute-start | bytes 12296 | tf_op jit(solution)/shard_map/ppermute | solution.py:14
  73.0 0.5 fusion
  73.5 6.4 %collective-permute-start.1 = (f32[1,2,512]{2,0,1:T(1,128)S(1)}, f32[1,2,512]{2,0,1:T(1,128)S(1)}, u32[]{:S(2)}, u32[]{:S(2)}) collective-permute-start(f32[1,2,512]{2,0,1:T(1,128)S(1)} %bitcast.40), channel_id=1, source_target_pairs={{1,0},{2,1},{3,2},{4,3},{5,4},{6,5},{7,6},{8,7},{9,8},{10,9},{11,1... | collective-permute-start | bytes 12296 | tf_op jit(solution)/shard_map/ppermute | solution.py:17
  79.9 0.0 collective-permute-done
  79.9 0.1 scatter-add.6
  80.0 1.2 collective-permute-done.1
  81.2 0.1 scatter-add.9
  81.3 0.0 copy-start
  81.3 0.8 copy-done
  82.1 0.0 reduce-scatter.2.cloned.1.call-update
  82.1 40.4 %reduce-scatter.2.cloned.1.call-done = f32[16,2,512]{2,0,1:T(8,128)} async-done(((f32[128,2,512]{2,0,1:T(8,128)}), f32[16,2,512]{2,0,1:T(8,128)}) %reduce-scatter.2.cloned.1.call-update) | async-done | bytes 65552 | tf_op jit(solution)/shard_map/reduce_scatter | solution.py:61
  122.5 1.4 %fusion.3 = (f32[1,16,512]{2,1,0:T(8,128)}, f32[1,16,512]{2,1,0:T(8,128)}) fusion(f32[16,2,512]{2,0,1:T(8,128)} %reduce-scatter.2.cloned.1.call-done), kind=kLoop, calls=%fused_computation.6 | loop fusion | flops 16384 | bytes 131072 | tf_op jit(solution)/shard_map/div | solution.py:63
  (8 shorter events, 0.1 us)
Async XLA Ops:
  7.2 57.7 %all-gather.2.cloned.1.call-start = ((), (), s32[]{:S(2)}) async-start(), calls=%async_computation.1 | async-start | bytes 1081344 | tf_op jit(solution)/shard_map/all_gather | solution.py:33
  8.6 113.8 %reduce-scatter.2.cloned.1.call-start = ((), (), s32[]{:S(2)}) async-start(), calls=%async_computation.2 | async-start | bytes 589824 | tf_op jit(solution)/shard_map/reduce_scatter | solution.py:61
  70.8 9.1 %collective-permute-start = (f32[1,2,512]{2,0,1:T(1,128)S(1)}, f32[1,2,512]{2,0,1:T(1,128)S(1)}, u32[]{:S(2)}, u32[]{:S(2)}) collective-permute-start(f32[1,2,512]{2,0,1:T(1,128)S(1)} %bitcast.41), channel_id=1, source_target_pairs={{0,1},{1,2},{2,3},{3,4},{4,5},{5,6},{6,7},{7,8},{8,9},{9,10},{10,1... | collective-permute-start | bytes 12296 | tf_op jit(solution)/shard_map/ppermute | solution.py:14
  73.5 7.7 %collective-permute-start.1 = (f32[1,2,512]{2,0,1:T(1,128)S(1)}, f32[1,2,512]{2,0,1:T(1,128)S(1)}, u32[]{:S(2)}, u32[]{:S(2)}) collective-permute-start(f32[1,2,512]{2,0,1:T(1,128)S(1)} %bitcast.40), channel_id=1, source_target_pairs={{1,0},{2,1},{3,2},{4,3},{5,4},{6,5},{7,6},{8,7},{9,8},{10,9},{11,1... | collective-permute-start | bytes 12296 | tf_op jit(solution)/shard_map/ppermute | solution.py:17
  81.3 0.8 copy-start
Sparse Core Ops, SparseCore 0:
  11.0 53.7 all-gather.1
  82.2 40.1 reduce-scatter.1
where the time goes:
time: 131 us
  waiting for transfers between devices  93.5 us (71%)
  between operations  14.1 us (11%)
  starting transfers between devices  8.65 us (7%)
  other arithmetic  6.26 us (5%)
  local copies, waits for them, and re-layouts  4.63 us (4%)
  matrix products  3.52 us (3%)
    all_gather x1, waiting for transfers between devices, on_device(): gathered = lax.all_gather(local_rows, 'brick', axis=1, tiled=True)  51.9 us
    reduce_scatter x1, waiting for transfers between devices, on_device(): lax.psum_scatter(interior, 'frame', scatter_dimension=0, tiled=True)  40.4 us
    ppermute x1, starting transfers between devices, extended(): lax.ppermute(lax.slice_in_dim(block, 0, width, axis=dim), axis, backward)  6.43 us
    dot_general x1, matrix products, on_device(): jnp.einsum('edb,eba->eda', rows_per_slot, divided_blocks, preferred_eleme...  2.83 us
    unnamed x2, other arithmetic  2.69 us
  transfers between devices with their start and end apart: 4, of which 3 were waited for; matrix products, arithmetic and copies ran while one was open for 4% of the time, Pallas kernels for 0%

commit v1 on v0

v1 whole, which is shorter than its diff:
```python
import functools

import jax
import jax.numpy as jnp
from jax import lax
from jax.experimental import pallas as pl
from jax.experimental.pallas import tpu as pltpu
from jax.sharding import PartitionSpec as P

MESH = pl.DeviceIdType.MESH
CAP = 4
FR_DEV = 4
MAXB = 8
PB_DEV = 16
ROWS_DEV = 16
SLOTS = FR_DEV * MAXB
PIX = 128
VOX = 512
HALVES = 2
WIDTH = VOX // HALVES
CHUNKS = 4


def iota(shape, dim):
    return lax.broadcasted_iota(jnp.int32, shape, dim)


def kernel(
    bricks,
    groups,
    pix_ref,
    vox_ref,
    count_ref,
    intensity_hbm,
    correction_hbm,
    split_hbm,
    merged_ref,
    weight_ref,
    inten,
    corr,
    split,
    request,
    packed,
    received,
    rowbuf,
    lhs,
    acc,
    partial,
    total,
    over_send,
    over_recv,
    load_sem,
    split_sem,
    req_send,
    req_recv,
    data_send,
    data_recv,
    sum_send,
    sum_recv,
    low_send,
    high_send,
    over_sem,
):
    me_f = lax.axis_index("frame")
    me_b = lax.axis_index("brick")
    barrier = pltpu.get_barrier_semaphore()

    def brick_peer(i):
        return lax.rem(me_b + i, bricks)

    def frame_peer(i):
        return lax.rem(me_f + i, groups)

    def greet_brick(i, carry):
        pl.semaphore_signal(
            barrier, inc=1, device_id={"brick": brick_peer(i)}, device_id_type=MESH
        )
        return carry

    def greet_frame(i, carry):
        pl.semaphore_signal(
            barrier, inc=1, device_id={"frame": frame_peer(i)}, device_id_type=MESH
        )
        return carry

    lax.fori_loop(1, bricks, greet_brick, 0)
    lax.fori_loop(1, groups, greet_frame, 0)

    loads = [
        pltpu.make_async_copy(intensity_hbm, inten, load_sem.at[0]),
        pltpu.make_async_copy(correction_hbm, corr, load_sem.at[1]),
    ]
    depth = SLOTS * PIX // CHUNKS
    splits = [
        pltpu.make_async_copy(
            split_hbm.at[pl.ds(k * depth, depth)],
            split.at[pl.ds(k * depth, depth)],
            split_sem.at[k],
        )
        for k in range(CHUNKS)
    ]
    for copy in loads + splits:
        copy.start()

    lane = iota((1, PIX), 1)
    row = jnp.full((1, PIX), -1, jnp.int32)
    for s in range(SLOTS):
        row = jnp.where(lane == s, pix_ref[s // MAXB, 0, s % MAXB], row)
    sub2, lane2 = iota((SLOTS, PIX), 0), iota((SLOTS, PIX), 1)
    column = jnp.sum(
        jnp.where(sub2 == lane2, jnp.broadcast_to(row, (SLOTS, PIX)), 0), axis=1, keepdims=True
    )
    same = (jnp.broadcast_to(row >> 4, (SLOTS, PIX)) == (column >> 4)).astype(jnp.int32)
    rank_row = jnp.sum(jnp.where(sub2 < lane2, same, 0), axis=0, keepdims=True)
    rank_col = jnp.sum(jnp.where(lane2 < sub2, same, 0), axis=1, keepdims=True)
    code = ((row >> 4) * CAP + rank_row) * 64 + (lane >> 3) * PB_DEV + (row & 15)
    request[me_b] = jnp.where(lane < SLOTS, code, -1)
    key = (column >> 4) * CAP + rank_col
    wide = iota((SLOTS, bricks * 2 * CAP), 1)
    pick = jnp.concatenate(
        [
            jnp.where(wide == key * 2 + c, 1.0, 0.0).astype(jnp.float32)
            for c in range(2)
        ],
        axis=0,
    ).astype(jnp.bfloat16)

    pl.semaphore_wait(barrier, bricks - 1 + groups - 1)

    def send_request(i, carry):
        pltpu.make_async_remote_copy(
            src_ref=request.at[me_b],
            dst_ref=request.at[me_b],
            send_sem=req_send,
            recv_sem=req_recv,
            device_id={"brick": brick_peer(i)},
            device_id_type=MESH,
        ).start()
        return carry

    lax.fori_loop(1, bricks, send_request, 0)

    for copy in loads:
        copy.wait()
    own = jnp.concatenate(
        [inten[...].reshape(FR_DEV * PB_DEV, PIX), corr[...].reshape(FR_DEV * PB_DEV, PIX)],
        axis=0,
    ).astype(jnp.bfloat16)

    def all_of(buffer, sem):
        others = buffer.at[pl.ds(0, bricks - 1)]
        return pltpu.make_async_copy(others, others, sem)

    all_of(request, req_recv).wait()

    asked = jnp.broadcast_to(request[...], (bricks, 2 * CAP, PIX))
    place = iota((bricks, 2 * CAP, PIX), 1)
    lane3 = iota((bricks, 2 * CAP, PIX), 2)
    wanted = (asked >> 6) == me_b * CAP + (place >> 1)
    found = jnp.sum(jnp.where(wanted, (asked & 63) + 1, 0), axis=2, keepdims=True)
    chosen = jnp.where(
        (found > 0) & (lane3 == (place & 1) * 64 + found - 1), 1.0, 0.0
    ).astype(jnp.float32)
    select = chosen.reshape(bricks * 2 * CAP, PIX).astype(jnp.bfloat16)
    blocks = jnp.dot(select, own, preferred_element_type=jnp.float32)
    packed[...] = blocks.reshape(bricks, 2 * CAP, PIX).astype(jnp.bfloat16)

    def send_data(i, carry):
        peer = brick_peer(i)
        pltpu.make_async_remote_copy(
            src_ref=packed.at[peer],
            dst_ref=received.at[me_b],
            send_sem=data_send,
            recv_sem=data_recv,
            device_id={"brick": peer},
            device_id_type=MESH,
        ).start()
        return carry

    lax.fori_loop(1, bricks, send_data, 0)
    received[me_b] = packed[me_b]
    all_of(received, data_recv).wait()

    table = received[...].astype(jnp.float32).reshape(bricks * 2 * CAP, PIX).astype(jnp.bfloat16)
    rowbuf[...] = jnp.dot(pick, table, preferred_element_type=jnp.float32)

    inner = groups * ROWS_DEV
    for copy in splits:
        copy.wait()

    def place_slot(f, m, carry):
        s = f * MAXB + m
        offset = vox_ref[f, 0, m]
        target = jnp.where(offset == 0, inner, jnp.where(offset == inner + 1, inner + 1, offset - 1))
        target = jnp.where(m < count_ref[f, 0], target, -1)
        hit = iota((inner + 8, PIX), 0) == target
        start = pl.multiple_of(s * PIX, PIX)
        parts = []
        for c in range(2):
            value = jnp.broadcast_to(rowbuf[pl.ds(c * SLOTS + s, 1), :], (inner + 8, PIX))
            parts.append(jnp.where(hit, value, 0.0))
        for g in range(groups):
            for c in range(2):
                lhs[pl.ds((2 * g + c) * ROWS_DEV, ROWS_DEV), pl.ds(start, PIX)] = parts[c][
                    g * ROWS_DEV : (g + 1) * ROWS_DEV
                ].astype(jnp.bfloat16)
        lhs[pl.ds(2 * inner, 16), pl.ds(start, PIX)] = jnp.concatenate(
            [part[inner:] for part in parts], axis=0
        ).astype(jnp.bfloat16)
        return carry

    def place_frame(f, carry):
        return lax.fori_loop(0, MAXB, functools.partial(place_slot, f), carry)

    lax.fori_loop(0, FR_DEV, place_frame, 0)

    def sum_copy(half, i):
        peer = frame_peer(i)
        return pltpu.make_async_remote_copy(
            src_ref=acc.at[half, pl.ds(peer * 2 * ROWS_DEV, 2 * ROWS_DEV)],
            dst_ref=partial.at[half, me_f],
            send_sem=sum_send.at[half],
            recv_sem=sum_recv.at[half],
            device_id={"frame": peer},
            device_id_type=MESH,
        )

    for half in range(HALVES):
        columns = pl.ds(half * WIDTH, WIDTH)
        acc[half] = jnp.dot(lhs[...], split[:, columns], preferred_element_type=jnp.float32)

        def send_sum(i, carry):
            sum_copy(half, i).start()
            return carry

        lax.fori_loop(1, groups, send_sum, 0)

    for side in range(2):
        for c in range(2):
            for n in range(VOX // PIX):
                half, at = n * PIX // WIDTH, n * PIX % WIDTH
                over_send[side, pl.ds(c * (VOX // PIX) + n, 1), :] = acc[
                    half, pl.ds(2 * inner + c * 8 + side, 1), pl.ds(at, PIX)
                ]

    def over_copy(side, step, owner, sem):
        return pltpu.make_async_remote_copy(
            src_ref=over_send.at[side],
            dst_ref=over_recv.at[me_f],
            send_sem=sem,
            recv_sem=over_sem,
            device_id={"frame": owner, "brick": brick_peer(step)},
            device_id_type=MESH,
        )

    low = over_copy(0, bricks - 1, groups - 1, low_send)
    high = over_copy(1, 1, 0, high_send)

    @pl.when(me_b > 0)
    def _():
        low.start()

    @pl.when(me_b < bricks - 1)
    def _():
        high.start()

    for half in range(HALVES):
        columns = pl.ds(half * WIDTH, WIDTH)
        others = partial.at[half, pl.ds(0, groups - 1)]
        partial[half, me_f] = acc[half, pl.ds(pl.multiple_of(me_f * 2 * ROWS_DEV, 32), 2 * ROWS_DEV), :]
        pltpu.make_async_copy(others, others, sum_recv.at[half]).wait()
        value = partial[half, 0]
        for g in range(1, groups):
            value = value + partial[half, g]
        total[:, columns] = value

    def take_overhang(at):
        pltpu.make_async_copy(over_recv, over_recv, over_sem).wait()
        value = over_recv[0]
        for g in range(1, groups):
            value = value + over_recv[g]
        for c in range(2):
            for n in range(VOX // PIX):
                where = (pl.ds(c * ROWS_DEV + at, 1), pl.ds(n * PIX, PIX))
                total[where] = total[where] + value[c * (VOX // PIX) + n : c * (VOX // PIX) + n + 1]

    @pl.when((me_f == groups - 1) & (me_b < bricks - 1))
    def _():
        take_overhang(ROWS_DEV - 1)

    @pl.when((me_f == 0) & (me_b > 0))
    def _():
        take_overhang(0)

    weight = total[pl.ds(ROWS_DEV, ROWS_DEV), :]
    weight_ref[...] = weight
    merged_ref[...] = total[pl.ds(0, ROWS_DEV), :] / jnp.maximum(weight, 1.0)

    all_of(request, req_send).wait()
    all_of(packed, data_send).wait()
    for half in range(HALVES):
        others = partial.at[half, pl.ds(0, groups - 1)]
        pltpu.make_async_copy(others, others, sum_send.at[half]).wait()

    @pl.when(me_b > 0)
    def _():
        low.wait_send()

    @pl.when(me_b < bricks - 1)
    def _():
        high.wait_send()


def on_device(intensity, correction, splitting, block_count, pix_index, vox_offset):
    bricks = lax.axis_size("brick")
    groups = lax.axis_size("frame")
    inner = groups * ROWS_DEV
    rows = 2 * inner + 16
    smem = pl.BlockSpec(memory_space=pltpu.SMEM)
    hbm = pl.BlockSpec(memory_space=pl.ANY)
    vmem = pl.BlockSpec(memory_space=pltpu.VMEM)
    dma = pltpu.SemaphoreType.DMA
    merged, weight = pl.pallas_call(
        functools.partial(kernel, bricks, groups),
        out_shape=[jax.ShapeDtypeStruct((ROWS_DEV, VOX), jnp.float32)] * 2,
        in_specs=[smem, smem, smem, hbm, hbm, hbm],
        out_specs=[vmem, vmem],
        scratch_shapes=[
            pltpu.VMEM((FR_DEV, PB_DEV, PIX), jnp.float32),
            pltpu.VMEM((FR_DEV, PB_DEV, PIX), jnp.float32),
            pltpu.VMEM((SLOTS * PIX, VOX), jnp.bfloat16),
            pltpu.VMEM((bricks, 1, PIX), jnp.int32),
            pltpu.VMEM((bricks, 2 * CAP, PIX), jnp.bfloat16),
            pltpu.VMEM((bricks, 2 * CAP, PIX), jnp.bfloat16),
            pltpu.VMEM((2 * SLOTS, PIX), jnp.float32),
            pltpu.VMEM((rows, SLOTS * PIX), jnp.bfloat16),
            pltpu.VMEM((HALVES, rows, WIDTH), jnp.float32),
            pltpu.VMEM((HALVES, groups, 2 * ROWS_DEV, WIDTH), jnp.float32),
            pltpu.VMEM((2 * ROWS_DEV, VOX), jnp.float32),
            pltpu.VMEM((2, 8, PIX), jnp.float32),
            pltpu.VMEM((groups, 8, PIX), jnp.float32),
            dma((2,)),
            dma((CHUNKS,)),
            dma,
            dma,
            dma,
            dma,
            dma((HALVES,)),
            dma((HALVES,)),
            dma,
            dma,
            dma,
        ],
        compiler_params=pltpu.CompilerParams(
            collective_id=0, has_side_effects=True, vmem_limit_bytes=32 * 1024 * 1024
        ),
    )(
        pix_index,
        vox_offset,
        block_count,
        intensity,
        correction,
        splitting.reshape(SLOTS * PIX, VOX),
    )
    return (merged[None], weight[None])


def solution(mesh):
    placed = (
        P("frame", "brick", None),
        P("frame", "brick", None),
        P("frame", "brick", None, None, None),
        P("frame", "brick"),
        P("frame", "brick", None),
        P("frame", "brick", None),
    )
    return jax.shard_map(
        on_device,
        mesh=mesh,
        in_specs=placed,
        out_specs=(P("brick", "frame", None), P("brick", "frame", None)),
        check_vma=False,
    )
```

time: 131 us -> 43.8 us (0.33)
  the two profiles are of different devices: /device:TPU:8 before, /device:TPU:1 now
where the time goes in v1:
time: 43.8 us; the launch traced here: 43.5 us
  Pallas kernels  35.9 us (82%)
  local copies, waits for them, and re-layouts  7.04 us (16%)
  between operations  0.64 us (1%)
    pallas_call x1, Pallas kernels, on_device(): pl.pallas_call(functools.partial(kernel, bricks, groups), out_shape=[jax....  35.9 us
    unnamed x13, local copies, waits for them, and re-layouts  7.04 us

profile of v1, /device:TPU:1, one launch (start us, length us, event | category | flops | bytes accessed | tf_op | source)
XLA Modules:
  0.0 43.5 jit_solution(3389210326350400393)
XLA Ops:
  0.6 0.7 %copy.8.count_ref = s32[4,1]{1,0:T(4,128)S(1)} copy(s32[4,1]{0,1:T(1,128)} %param.9) | data formatting | bytes 32 | tf_op args[3]
  1.4 0.0 copy-start
  1.4 2.2 %copy-done = bf16[4,1,8,128,512]{4,3,2,1,0:T(8,128)(2,1)S(1)} copy-done((bf16[4,1,8,128,512]{4,3,2,1,0:T(8,128)(2,1)S(1)}, bf16[4,1,8,128,512]{4,3,2,1,0:T(8,128)(2,1)}, u32[]{:S(2)}) %copy-start) | copy-done | bytes 4194328
  3.6 0.0 copy-start.1
  3.6 0.8 %copy-done.1 = f32[4,16,128]{2,1,0:T(8,128)S(1)} copy-done((f32[4,16,128]{2,1,0:T(8,128)S(1)}, f32[4,16,128]{2,1,0:T(8,128)}, u32[]{:S(2)}) %copy-start.1) | copy-done | bytes 32792
  4.3 0.0 copy-start.2
  4.3 0.8 %copy-done.2 = f32[4,16,128]{2,1,0:T(8,128)S(1)} copy-done((f32[4,16,128]{2,1,0:T(8,128)S(1)}, f32[4,16,128]{2,1,0:T(8,128)}, u32[]{:S(2)}) %copy-start.2) | copy-done | bytes 32792
  5.1 0.0 copy-start.3
  5.1 0.7 %copy-done.3 = s32[4,1,8]{2,1,0:T(1,128)S(1)} copy-done((s32[4,1,8]{2,1,0:T(1,128)S(1)}, s32[4,1,8]{2,1,0:T(1,128)}, u32[]{:S(2)}) %copy-start.3) | copy-done | bytes 152
  5.8 0.0 copy-start.4
  5.8 0.7 %copy-done.4 = s32[4,1,8]{2,1,0:T(1,128)S(1)} copy-done((s32[4,1,8]{2,1,0:T(1,128)S(1)}, s32[4,1,8]{2,1,0:T(1,128)}, u32[]{:S(2)}) %copy-start.4) | copy-done | bytes 152
  6.4 35.9 %shard_map.77 = (f32[16,512]{1,0:T(8,128)S(1)}, f32[16,512]{1,0:T(8,128)S(1)}) custom-call(s32[4,1,8]{2,1,0:T(1,128)S(1)} %copy-done.3, s32[4,1,8]{2,1,0:T(1,128)S(1)} %copy-done.4, s32[4,1]{1,0:T(4,128)S(1)} %copy.8.count_ref, f32[4,16,128]{2,1,0:T(8,128)S(1)} %copy-done.1, f32[4,16,128]{2,1,0:T(8,128)S(1)} %copy-done.2, bf16[4096,512]{1,0:T(8,128)(2,1)S(1)} %bitcast.3), custom_call_target="tpu_custom_call" | custom-call | tf_op jit(solution)/shard_map/pallas_call | solution.py:323
  42.3 0.6 %copy.11 = f32[1,16,512]{2,1,0:T(8,128)} copy(f32[1,16,512]{2,1,0:T(8,128)S(1)} %bitcast.5) | data formatting | bytes 65536
  42.9 0.6 %copy.12 = f32[1,16,512]{2,1,0:T(8,128)} copy(f32[1,16,512]{2,1,0:T(8,128)S(1)} %bitcast.4) | data formatting | bytes 65536
Async XLA Ops:
  1.4 2.2 %copy-start = (bf16[4,1,8,128,512]{4,3,2,1,0:T(8,128)(2,1)S(1)}, bf16[4,1,8,128,512]{4,3,2,1,0:T(8,128)(2,1)}, u32[]{:S(2)}) copy-start(bf16[4,1,8,128,512]{4,3,2,1,0:T(8,128)(2,1)} %param.8) | copy-start | bytes 12582916
  3.6 0.8 %copy-start.1 = (f32[4,16,128]{2,1,0:T(8,128)S(1)}, f32[4,16,128]{2,1,0:T(8,128)}, u32[]{:S(2)}) copy-start(f32[4,16,128]{2,1,0:T(8,128)} %intensity_hbm.1) | copy-start | bytes 98308
  4.3 0.8 %copy-start.2 = (f32[4,16,128]{2,1,0:T(8,128)S(1)}, f32[4,16,128]{2,1,0:T(8,128)}, u32[]{:S(2)}) copy-start(f32[4,16,128]{2,1,0:T(8,128)} %correction_hbm.1) | copy-start | bytes 98308
  5.1 0.7 %copy-start.3 = (s32[4,1,8]{2,1,0:T(1,128)S(1)}, s32[4,1,8]{2,1,0:T(1,128)}, u32[]{:S(2)}) copy-start(s32[4,1,8]{2,1,0:T(1,128)} %pix_ref.1) | copy-start | bytes 388
  5.8 0.7 %copy-start.4 = (s32[4,1,8]{2,1,0:T(1,128)S(1)}, s32[4,1,8]{2,1,0:T(1,128)}, u32[]{:S(2)}) copy-start(s32[4,1,8]{2,1,0:T(1,128)} %vox_ref.1) | copy-start | bytes 388

commit v2 on v1

v2 whole, which is shorter than its diff:
```python
import functools

import jax
import jax.numpy as jnp
from jax import lax
from jax.experimental import pallas as pl
from jax.experimental.pallas import tpu as pltpu
from jax.sharding import PartitionSpec as P

MESH = pl.DeviceIdType.MESH
CAP = 4
FR_DEV = 4
MAXB = 8
PB_DEV = 16
ROWS_DEV = 16
SLOTS = FR_DEV * MAXB
PIX = 128
VOX = 512
HALVES = 2
WIDTH = VOX // HALVES
CHUNKS = 4
NEAR = 8


def iota(shape, dim):
    return lax.broadcasted_iota(jnp.int32, shape, dim)


def kernel(
    bricks,
    groups,
    pix_hbm,
    vox_hbm,
    count_hbm,
    intensity_hbm,
    correction_hbm,
    split_hbm,
    total,
    pix_ref,
    vox_ref,
    count_ref,
    inten,
    corr,
    split,
    pixels,
    request,
    packed,
    received,
    rowbuf,
    lhs,
    acc,
    partial,
    over_send,
    over_recv,
    load_sem,
    split_sem,
    pix_send,
    pix_recv,
    req_send,
    req_recv,
    data_send,
    data_recv,
    sum_send,
    sum_recv,
    over_send_sem,
    over_sem,
):
    me_f = lax.axis_index("frame")
    me_b = lax.axis_index("brick")
    far = bricks // NEAR
    me_far = me_b // NEAR
    me_near = me_b - me_far * NEAR
    held = CAP * far
    barrier = pltpu.get_barrier_semaphore()

    def brick_peer(i):
        return lax.rem(me_b + i, bricks)

    def near_index(i):
        return lax.rem(me_near + i, NEAR)

    def near_peer(i):
        return me_far * NEAR + near_index(i)

    def frame_peer(i):
        return lax.rem(me_f + i, groups)

    for i in range(1, far):
        pl.semaphore_signal(
            barrier, inc=1, device_id={"brick": brick_peer(i * NEAR)}, device_id_type=MESH
        )
    for i in range(1, NEAR):
        pl.semaphore_signal(
            barrier, inc=1, device_id={"brick": near_peer(i)}, device_id_type=MESH
        )
    for i in range(1, groups):
        pl.semaphore_signal(
            barrier, inc=1, device_id={"frame": frame_peer(i)}, device_id_type=MESH
        )

    tables = [
        pltpu.make_async_copy(pix_hbm, pix_ref, load_sem.at[0]),
        pltpu.make_async_copy(vox_hbm, vox_ref, load_sem.at[1]),
        pltpu.make_async_copy(count_hbm, count_ref, load_sem.at[2]),
    ]
    loads = [
        pltpu.make_async_copy(intensity_hbm, inten, load_sem.at[3]),
        pltpu.make_async_copy(correction_hbm, corr, load_sem.at[4]),
    ]
    depth = SLOTS * PIX // CHUNKS
    splits = [
        pltpu.make_async_copy(
            split_hbm.at[pl.ds(k * depth, depth)],
            split.at[pl.ds(k * depth, depth)],
            split_sem.at[k],
        )
        for k in range(CHUNKS)
    ]
    for copy in tables + loads + splits:
        copy.start()
    for copy in tables:
        copy.wait()

    lane = iota((1, PIX), 1)
    row = jnp.full((1, PIX), -1, jnp.int32)
    for s in range(SLOTS):
        row = jnp.where(lane == s, pix_ref[s // MAXB, 0, s % MAXB], row)
    sub2, lane2 = iota((SLOTS, PIX), 0), iota((SLOTS, PIX), 1)
    column = jnp.sum(
        jnp.where(sub2 == lane2, jnp.broadcast_to(row, (SLOTS, PIX)), 0), axis=1, keepdims=True
    )
    near_row = (row >> 4) & (NEAR - 1)
    near_col = (column >> 4) & (NEAR - 1)
    same = (jnp.broadcast_to(near_row, (SLOTS, PIX)) == near_col).astype(jnp.int32)
    rank_row = jnp.sum(jnp.where(sub2 < lane2, same, 0), axis=0, keepdims=True)
    rank_col = jnp.sum(jnp.where(lane2 < sub2, same, 0), axis=1, keepdims=True)
    where_row = (row // (NEAR * PB_DEV)) * 128 + (lane >> 3) * PB_DEV + (row & 15)
    code = (near_row * held + rank_row) * 1024 + where_row
    request[me_near] = jnp.where(lane < SLOTS, code, -1)
    key = near_col * held + rank_col
    wide = iota((SLOTS, NEAR * 2 * held), 1)
    pick = jnp.concatenate(
        [jnp.where(wide == key * 2 + c, 1.0, 0.0).astype(jnp.float32) for c in range(2)],
        axis=0,
    ).astype(jnp.bfloat16)

    for copy in loads:
        copy.wait()
    pixels[me_far] = jnp.concatenate(
        [inten[...].reshape(FR_DEV * PB_DEV, PIX), corr[...].reshape(FR_DEV * PB_DEV, PIX)],
        axis=0,
    ).astype(jnp.bfloat16)

    pl.semaphore_wait(barrier, far - 1 + NEAR - 1 + groups - 1)

    for i in range(1, far):
        pltpu.make_async_remote_copy(
            src_ref=pixels.at[me_far],
            dst_ref=pixels.at[me_far],
            send_sem=pix_send,
            recv_sem=pix_recv,
            device_id={"brick": brick_peer(i * NEAR)},
            device_id_type=MESH,
        ).start()
    for i in range(1, NEAR):
        pltpu.make_async_remote_copy(
            src_ref=request.at[me_near],
            dst_ref=request.at[me_near],
            send_sem=req_send,
            recv_sem=req_recv,
            device_id={"brick": near_peer(i)},
            device_id_type=MESH,
        ).start()

    def others_of(buffer, count, sem):
        others = buffer.at[pl.ds(0, count - 1)]
        return pltpu.make_async_copy(others, others, sem)

    others_of(request, NEAR, req_recv).wait()

    asked = jnp.concatenate(
        [jnp.broadcast_to(request[d], (2 * held, PIX)) for d in range(NEAR)], axis=0
    )
    place = lax.rem(iota((NEAR * 2 * held, PIX), 0), 2 * held)
    wanted = (asked >> 10) == me_near * held + (place >> 1)
    found = jnp.sum(jnp.where(wanted, (asked & 1023) + 1, 0), axis=1, keepdims=True)
    spot = jnp.where(found > 0, found - 1 + (place[:, 0:1] & 1) * 64, -1)
    select = jnp.where(iota((NEAR * 2 * held, far * PIX), 1) == spot, 1.0, 0.0)
    select = select.astype(jnp.float32).astype(jnp.bfloat16)

    others_of(pixels, far, pix_recv).wait()
    blocks = jnp.dot(
        select, pixels[...].reshape(far * PIX, PIX), preferred_element_type=jnp.float32
    ).astype(jnp.bfloat16)
    packed[...] = blocks.reshape(NEAR, 2 * held, PIX)

    for i in range(1, NEAR):
        pltpu.make_async_remote_copy(
            src_ref=packed.at[near_index(i)],
            dst_ref=received.at[me_near],
            send_sem=data_send,
            recv_sem=data_recv,
            device_id={"brick": near_peer(i)},
            device_id_type=MESH,
        ).start()
    received[me_near] = packed[me_near]
    others_of(received, NEAR, data_recv).wait()

    rowbuf[...] = jnp.dot(
        pick, received[...].reshape(NEAR * 2 * held, PIX), preferred_element_type=jnp.float32
    )

    inner = groups * ROWS_DEV

    def place_slot(f, m, carry):
        s = f * MAXB + m
        offset = vox_ref[f, 0, m]
        target = jnp.where(offset == 0, inner, jnp.where(offset == inner + 1, inner + 1, offset - 1))
        target = jnp.where(m < count_ref[f], target, -1)
        hit = iota((inner + 8, PIX), 0) == target
        start = pl.multiple_of(s * PIX, PIX)
        parts = []
        for c in range(2):
            value = jnp.broadcast_to(rowbuf[pl.ds(c * SLOTS + s, 1), :], (inner + 8, PIX))
            parts.append(jnp.where(hit, value, 0.0))
        for g in range(groups):
            for c in range(2):
                lhs[pl.ds((2 * g + c) * ROWS_DEV, ROWS_DEV), pl.ds(start, PIX)] = parts[c][
                    g * ROWS_DEV : (g + 1) * ROWS_DEV
                ].astype(jnp.bfloat16)
        lhs[pl.ds(2 * inner, 16), pl.ds(start, PIX)] = jnp.concatenate(
            [part[inner:] for part in parts], axis=0
        ).astype(jnp.bfloat16)
        return carry

    def place_frame(f, carry):
        return lax.fori_loop(0, MAXB, functools.partial(place_slot, f), carry)

    lax.fori_loop(0, FR_DEV, place_frame, 0)
    for copy in splits:
        copy.wait()

    def over_copy(side, half, step, owner):
        return pltpu.make_async_remote_copy(
            src_ref=over_send.at[side, half],
            dst_ref=over_recv.at[half, me_f],
            send_sem=over_send_sem.at[side],
            recv_sem=over_sem,
            device_id={"frame": owner, "brick": brick_peer(step)},
            device_id_type=MESH,
        )

    parts = WIDTH // PIX
    for half in range(HALVES):
        columns = pl.ds(half * WIDTH, WIDTH)
        acc[half] = jnp.dot(lhs[...], split[:, columns], preferred_element_type=jnp.float32)

        for side in range(2):
            for c in range(2):
                for n in range(parts):
                    over_send[side, half, pl.ds(c * parts + n, 1), :] = acc[
                        half, pl.ds(2 * inner + c * 8 + side, 1), pl.ds(n * PIX, PIX)
                    ]

        @pl.when(me_b > 0)
        def _():
            over_copy(0, half, bricks - 1, groups - 1).start()

        @pl.when(me_b < bricks - 1)
        def _():
            over_copy(1, half, 1, 0).start()

        for i in range(1, groups):
            peer = frame_peer(i)
            pltpu.make_async_remote_copy(
                src_ref=acc.at[half, pl.ds(peer * 2 * ROWS_DEV, 2 * ROWS_DEV)],
                dst_ref=partial.at[half, me_f],
                send_sem=sum_send.at[half],
                recv_sem=sum_recv.at[half],
                device_id={"frame": peer},
                device_id_type=MESH,
            ).start()
        partial[half, me_f] = acc[
            half, pl.ds(pl.multiple_of(me_f * 2 * ROWS_DEV, 2 * ROWS_DEV), 2 * ROWS_DEV), :
        ]

    for half in range(HALVES):
        columns = pl.ds(half * WIDTH, WIDTH)
        others = partial.at[half, pl.ds(0, groups - 1)]
        pltpu.make_async_copy(others, others, sum_recv.at[half]).wait()
        value = partial[half, 0]
        for g in range(1, groups):
            value = value + partial[half, g]
        total[:, columns] = value

    def take_overhang(at):
        pltpu.make_async_copy(over_recv, over_recv, over_sem).wait()
        for half in range(HALVES):
            value = over_recv[half, 0]
            for g in range(1, groups):
                value = value + over_recv[half, g]
            for c in range(2):
                for n in range(parts):
                    where = (pl.ds(c * ROWS_DEV + at, 1), pl.ds(half * WIDTH + n * PIX, PIX))
                    total[where] = total[where] + value[c * parts + n : c * parts + n + 1]

    @pl.when((me_f == groups - 1) & (me_b < bricks - 1))
    def _():
        take_overhang(ROWS_DEV - 1)

    @pl.when((me_f == 0) & (me_b > 0))
    def _():
        take_overhang(0)

    others_of(pixels, far, pix_send).wait()
    others_of(request, NEAR, req_send).wait()
    others_of(packed, NEAR, data_send).wait()
    for half in range(HALVES):
        others = partial.at[half, pl.ds(0, groups - 1)]
        pltpu.make_async_copy(others, others, sum_send.at[half]).wait()

    def sent_over(side):
        pltpu.make_async_copy(over_send.at[side], over_send.at[side], over_send_sem.at[side]).wait()

    @pl.when(me_b > 0)
    def _():
        sent_over(0)

    @pl.when(me_b < bricks - 1)
    def _():
        sent_over(1)


def on_device(intensity, correction, splitting, block_count, pix_index, vox_offset):
    bricks = lax.axis_size("brick")
    groups = lax.axis_size("frame")
    far = bricks // NEAR
    message = 2 * CAP * far
    rows = 2 * groups * ROWS_DEV + 16
    hbm = pl.BlockSpec(memory_space=pltpu.HBM)
    dma = pltpu.SemaphoreType.DMA
    total = pl.pallas_call(
        functools.partial(kernel, bricks, groups),
        out_shape=jax.ShapeDtypeStruct((2 * ROWS_DEV, VOX), jnp.float32),
        in_specs=[hbm] * 6,
        out_specs=pl.BlockSpec(memory_space=pltpu.VMEM),
        scratch_shapes=[
            pltpu.SMEM((FR_DEV, 1, MAXB), jnp.int32),
            pltpu.SMEM((FR_DEV, 1, MAXB), jnp.int32),
            pltpu.SMEM((FR_DEV,), jnp.int32),
            pltpu.VMEM((FR_DEV, PB_DEV, PIX), jnp.float32),
            pltpu.VMEM((FR_DEV, PB_DEV, PIX), jnp.float32),
            pltpu.VMEM((SLOTS * PIX, VOX), jnp.bfloat16),
            pltpu.VMEM((far, 2 * FR_DEV * PB_DEV, PIX), jnp.bfloat16),
            pltpu.VMEM((NEAR, 1, PIX), jnp.int32),
            pltpu.VMEM((NEAR, message, PIX), jnp.bfloat16),
            pltpu.VMEM((NEAR, message, PIX), jnp.bfloat16),
            pltpu.VMEM((2 * SLOTS, PIX), jnp.float32),
            pltpu.VMEM((rows, SLOTS * PIX), jnp.bfloat16),
            pltpu.VMEM((HALVES, rows, WIDTH), jnp.float32),
            pltpu.VMEM((HALVES, groups, 2 * ROWS_DEV, WIDTH), jnp.float32),
            pltpu.VMEM((2, HALVES, 2 * WIDTH // PIX, PIX), jnp.float32),
            pltpu.VMEM((HALVES, groups, 2 * WIDTH // PIX, PIX), jnp.float32),
            dma((5,)),
            dma((CHUNKS,)),
            dma,
            dma,
            dma,
            dma,
            dma,
            dma,
            dma((HALVES,)),
            dma((HALVES,)),
            dma((2,)),
            dma,
        ],
        compiler_params=pltpu.CompilerParams(
            collective_id=0, has_side_effects=True, vmem_limit_bytes=60 * 1024 * 1024
        ),
    )(
        pix_index,
        vox_offset,
        block_count.reshape(FR_DEV),
        intensity,
        correction,
        splitting.reshape(SLOTS * PIX, VOX),
    )
    weight = total[ROWS_DEV:]
    merged = total[:ROWS_DEV] / jnp.maximum(weight, 1.0)
    return (merged[None], weight[None])


def solution(mesh):
    placed = (
        P("frame", "brick", None),
        P("frame", "brick", None),
        P("frame", "brick", None, None, None),
        P("frame", "brick"),
        P("frame", "brick", None),
        P("frame", "brick", None),
    )
    return jax.shard_map(
        on_device,
        mesh=mesh,
        in_specs=placed,
        out_specs=(P("brick", "frame", None), P("brick", "frame", None)),
        check_vma=False,
    )
```

time: 43.8 us -> 32.7 us (0.75)
  local copies, waits for them, and re-layouts: 7.04 us -> 0 us
  Pallas kernels: 35.9 us -> 30.5 us
  other arithmetic: 0 us -> 1.41 us
    unnamed x13 -> x0, local copies, waits for them, and re-layouts: 7.04 us -> none
    pallas_call x1, Pallas kernels: 35.9 us -> 30.5 us  [on_device(): pl.pallas_call(functools.partial(kernel, bricks, groups), out_shape=jax.S...]
    broadcast_in_dim x0 -> x1, other arithmetic: none -> 1.41 us  [on_device(): return (merged[None], weight[None])]
where the time goes in v2:
time: 32.7 us; the launch traced here: 32.6 us
  Pallas kernels  30.5 us (93%)
  other arithmetic  1.41 us (4%)
  between operations  0.64 us (2%)
    pallas_call x1, Pallas kernels, on_device(): pl.pallas_call(functools.partial(kernel, bricks, groups), out_shape=jax.S...  30.5 us
    broadcast_in_dim x1, other arithmetic, on_device(): return (merged[None], weight[None])  1.41 us

profile of v2, /device:TPU:1, one launch (start us, length us, event | category | flops | bytes accessed | tf_op | source)
XLA Modules:
  0.0 32.6 jit_solution(10580225261639683199)
XLA Ops:
  0.6 30.5 %shard_map.77 = f32[32,512]{1,0:T(8,128)} custom-call(s32[4,1,8]{2,1,0:T(1,128)} %pix_hbm.1, s32[4,1,8]{2,1,0:T(1,128)} %vox_hbm.1, s32[4]{0:T(128)} %bitcast.7, f32[4,16,128]{2,1,0:T(8,128)} %intensity_hbm.1, f32[4,16,128]{2,1,0:T(8,128)} %correction_hbm.1, bf16[4096,512]{1,0:T(8,128)(2,1)} %bitcast.6), custom_call_target="tpu_custom_call" | custom-call | tf_op jit(solution)/shard_map/pallas_call | solution.py:342
  31.2 1.4 %slice_bitcast_fusion = (f32[1,16,512]{2,1,0:T(8,128)}, f32[1,16,512]{2,1,0:T(8,128)}) fusion(f32[32,512]{1,0:T(8,128)} %shard_map.77), kind=kLoop, calls=%fused_computation.1 | loop fusion | flops 16384 | bytes 131072 | tf_op jit(solution)/shard_map/broadcast_in_dim | solution.py:390

commit v3 on v2

--- a/solution.py
+++ b/solution.py
@@ -19,7 +19,7 @@
 HALVES = 2
 WIDTH = VOX // HALVES
 CHUNKS = 4
-NEAR = 8
+FAR = 4
 
 
 def iota(shape, dim):
@@ -67,29 +67,37 @@
 ):
     me_f = lax.axis_index("frame")
     me_b = lax.axis_index("brick")
-    far = bricks // NEAR
-    me_far = me_b // NEAR
-    me_near = me_b - me_far * NEAR
-    held = CAP * far
+    near = bricks // FAR
+    me_y = me_b // (2 * FAR)
+    me_c = lax.rem(me_b, 2)
+    me_far = lax.rem(me_b // 2, FAR)
+    me_near = me_y * 2 + me_c
+    held = CAP * FAR
     barrier = pltpu.get_barrier_semaphore()
 
     def brick_peer(i):
         return lax.rem(me_b + i, bricks)
 
+    def brick_of(at_near, at_far):
+        return (at_near // 2 * FAR + at_far) * 2 + lax.rem(at_near, 2)
+
     def near_index(i):
-        return lax.rem(me_near + i, NEAR)
+        return lax.rem(me_near + i, near)
 
     def near_peer(i):
-        return me_far * NEAR + near_index(i)
+        return brick_of(near_index(i), me_far)
+
+    def far_peer(i):
+        return brick_of(me_near, lax.rem(me_far + i, FAR))
 
     def frame_peer(i):
         return lax.rem(me_f + i, groups)
 
-    for i in range(1, far):
+    for i in range(1, FAR):
         pl.semaphore_signal(
-            barrier, inc=1, device_id={"brick": brick_peer(i * NEAR)}, device_id_type=MESH
+            barrier, inc=1, device_id={"brick": far_peer(i)}, device_id_type=MESH
         )
-    for i in range(1, NEAR):
+    for i in range(1, near):
         pl.semaphore_signal(
             barrier, inc=1, device_id={"brick": near_peer(i)}, device_id_type=MESH
         )
@@ -129,16 +137,16 @@
     column = jnp.sum(
         jnp.where(sub2 == lane2, jnp.broadcast_to(row, (SLOTS, PIX)), 0), axis=1, keepdims=True
     )
-    near_row = (row >> 4) & (NEAR - 1)
-    near_col = (column >> 4) & (NEAR - 1)
+    near_row = (row // (2 * FAR * PB_DEV)) * 2 + ((row >> 4) & 1)
+    near_col = (column // (2 * FAR * PB_DEV)) * 2 + ((column >> 4) & 1)
     same = (jnp.broadcast_to(near_row, (SLOTS, PIX)) == near_col).astype(jnp.int32)
     rank_row = jnp.sum(jnp.where(sub2 < lane2, same, 0), axis=0, keepdims=True)
     rank_col = jnp.sum(jnp.where(lane2 < sub2, same, 0), axis=1, keepdims=True)
-    where_row = (row // (NEAR * PB_DEV)) * 128 + (lane >> 3) * PB_DEV + (row & 15)
+    where_row = ((row >> 5) & (FAR - 1)) * 128 + (lane >> 3) * PB_DEV + (row & 15)
     code = (near_row * held + rank_row) * 1024 + where_row
     request[me_near] = jnp.where(lane < SLOTS, code, -1)
     key = near_col * held + rank_col
-    wide = iota((SLOTS, NEAR * 2 * held), 1)
+    wide = iota((SLOTS, near * 2 * held), 1)
     pick = jnp.concatenate(
         [jnp.where(wide == key * 2 + c, 1.0, 0.0).astype(jnp.float32) for c in range(2)],
         axis=0,
@@ -151,18 +159,18 @@
         axis=0,
     ).astype(jnp.bfloat16)
 
-    pl.semaphore_wait(barrier, far - 1 + NEAR - 1 + groups - 1)
-
-    for i in range(1, far):
+    pl.semaphore_wait(barrier, FAR - 1 + near - 1 + groups - 1)
+
+    for i in range(1, FAR):
         pltpu.make_async_remote_copy(
             src_ref=pixels.at[me_far],
             dst_ref=pixels.at[me_far],
             send_sem=pix_send,
             recv_sem=pix_recv,
-            device_id={"brick": brick_peer(i * NEAR)},
+            device_id={"brick": far_peer(i)},
             device_id_type=MESH,
         ).start()
-    for i in range(1, NEAR):
+    for i in range(1, near):
         pltpu.make_async_remote_copy(
             src_ref=request.at[me_near],
             dst_ref=request.at[me_near],
@@ -176,25 +184,25 @@
         others = buffer.at[pl.ds(0, count - 1)]
         return pltpu.make_async_copy(others, others, sem)
 
-    others_of(request, NEAR, req_recv).wait()
+    others_of(request, near, req_recv).wait()
 
     asked = jnp.concatenate(
-        [jnp.broadcast_to(request[d], (2 * held, PIX)) for d in range(NEAR)], axis=0
-    )
-    place = lax.rem(iota((NEAR * 2 * held, PIX), 0), 2 * held)
+        [jnp.broadcast_to(request[d], (2 * held, PIX)) for d in range(near)], axis=0
+    )
+    place = lax.rem(iota((near * 2 * held, PIX), 0), 2 * held)
     wanted = (asked >> 10) == me_near * held + (place >> 1)
     found = jnp.sum(jnp.where(wanted, (asked & 1023) + 1, 0), axis=1, keepdims=True)
     spot = jnp.where(found > 0, found - 1 + (place[:, 0:1] & 1) * 64, -1)
-    select = jnp.where(iota((NEAR * 2 * held, far * PIX), 1) == spot, 1.0, 0.0)
+    select = jnp.where(iota((near * 2 * held, FAR * PIX), 1) == spot, 1.0, 0.0)
     select = select.astype(jnp.float32).astype(jnp.bfloat16)
 
-    others_of(pixels, far, pix_recv).wait()
+    others_of(pixels, FAR, pix_recv).wait()
     blocks = jnp.dot(
-        select, pixels[...].reshape(far * PIX, PIX), preferred_element_type=jnp.float32
+        select, pixels[...].reshape(FAR * PIX, PIX), preferred_element_type=jnp.float32
     ).astype(jnp.bfloat16)
-    packed[...] = blocks.reshape(NEAR, 2 * held, PIX)
-
-    for i in range(1, NEAR):
+    packed[...] = blocks.reshape(near, 2 * held, PIX)
+
+    for i in range(1, near):
         pltpu.make_async_remote_copy(
             src_ref=packed.at[near_index(i)],
             dst_ref=received.at[me_near],
@@ -204,10 +212,10 @@
             device_id_type=MESH,
         ).start()
     received[me_near] = packed[me_near]
-    others_of(received, NEAR, data_recv).wait()
+    others_of(received, near, data_recv).wait()
 
     rowbuf[...] = jnp.dot(
-        pick, received[...].reshape(NEAR * 2 * held, PIX), preferred_element_type=jnp.float32
+        pick, received[...].reshape(near * 2 * held, PIX), preferred_element_type=jnp.float32
     )
 
     inner = groups * ROWS_DEV
@@ -312,9 +320,9 @@
     def _():
         take_overhang(0)
 
-    others_of(pixels, far, pix_send).wait()
-    others_of(request, NEAR, req_send).wait()
-    others_of(packed, NEAR, data_send).wait()
+    others_of(pixels, FAR, pix_send).wait()
+    others_of(request, near, req_send).wait()
+    others_of(packed, near, data_send).wait()
     for half in range(HALVES):
         others = partial.at[half, pl.ds(0, groups - 1)]
         pltpu.make_async_copy(others, others, sum_send.at[half]).wait()
@@ -334,8 +342,8 @@
 def on_device(intensity, correction, splitting, block_count, pix_index, vox_offset):
     bricks = lax.axis_size("brick")
     groups = lax.axis_size("frame")
-    far = bricks // NEAR
-    message = 2 * CAP * far
+    near = bricks // FAR
+    message = 2 * CAP * FAR
     rows = 2 * groups * ROWS_DEV + 16
     hbm = pl.BlockSpec(memory_space=pltpu.HBM)
     dma = pltpu.SemaphoreType.DMA
@@ -351,10 +359,10 @@
             pltpu.VMEM((FR_DEV, PB_DEV, PIX), jnp.float32),
             pltpu.VMEM((FR_DEV, PB_DEV, PIX), jnp.float32),
             pltpu.VMEM((SLOTS * PIX, VOX), jnp.bfloat16),
-            pltpu.VMEM((far, 2 * FR_DEV * PB_DEV, PIX), jnp.bfloat16),
-            pltpu.VMEM((NEAR, 1, PIX), jnp.int32),
-            pltpu.VMEM((NEAR, message, PIX), jnp.bfloat16),
-            pltpu.VMEM((NEAR, message, PIX), jnp.bfloat16),
+            pltpu.VMEM((FAR, 2 * FR_DEV * PB_DEV, PIX), jnp.bfloat16),
+            pltpu.VMEM((near, 1, PIX), jnp.int32),
+            pltpu.VMEM((near, message, PIX), jnp.bfloat16),
+            pltpu.VMEM((near, message, PIX), jnp.bfloat16),
             pltpu.VMEM((2 * SLOTS, PIX), jnp.float32),
             pltpu.VMEM((rows, SLOTS * PIX), jnp.bfloat16),
             pltpu.VMEM((HALVES, rows, WIDTH), jnp.float32),
@@ -375,15 +383,20 @@
             dma,
         ],
         compiler_params=pltpu.CompilerParams(
-            collective_id=0, has_side_effects=True, vmem_limit_bytes=60 * 1024 * 1024
+            collective_id=0, has_side_effects=True, vmem_limit_bytes=32 * 1024 * 1024
         ),
     )(
-        pix_index,
-        vox_offset,
-        block_count.reshape(FR_DEV),
-        intensity,
-        correction,
-        splitting.reshape(SLOTS * PIX, VOX),
+        *[
+            pltpu.with_memory_space_constraint(x, pltpu.HBM)
+            for x in (
+                pix_index,
+                vox_offset,
+                block_count.reshape(FR_DEV),
+                intensity,
+                correction,
+                splitting.reshape(SLOTS * PIX, VOX),
+            )
+        ]
     )
     weight = total[ROWS_DEV:]
     merged = total[:ROWS_DEV] / jnp.maximum(weight, 1.0)

time: 32.7 us -> 31.8 us (0.972)
  other arithmetic: 1.41 us -> 0.63 us
    broadcast_in_dim x1, other arithmetic: 1.41 us -> 0.63 us  [on_device(): return (merged[None], weight[None])]
where the time goes in v3:
time: 31.8 us; the launch traced here: 31.7 us
  Pallas kernels  30.4 us (96%)
  between operations  0.64 us (2%)
  other arithmetic  0.63 us (2%)
    pallas_call x1, Pallas kernels, on_device(): pl.pallas_call(functools.partial(kernel, bricks, groups), out_shape=jax.S...  30.4 us

profile of v3, /device:TPU:1, one launch (start us, length us, event | category | flops | bytes accessed | tf_op | source)
XLA Modules:
  0.0 31.7 jit_solution(7423944448838880945)
XLA Ops:
  0.6 30.4 %shard_map.77 = f32[32,512]{1,0:T(8,128)S(1)} custom-call(s32[4,1,8]{2,1,0:T(1,128)} %pix_hbm.1, s32[4,1,8]{2,1,0:T(1,128)} %vox_hbm.1, s32[4]{0:T(128)} %bitcast.7, f32[4,16,128]{2,1,0:T(8,128)} %intensity_hbm.1, f32[4,16,128]{2,1,0:T(8,128)} %correction_hbm.1, bf16[4096,512]{1,0:T(8,128)(2,1)} %bitcast.6), custom_call_target="tpu_custom_call" | custom-call | tf_op jit(solution)/shard_map/pallas_call | solution.py:350
  31.1 0.6 %slice_bitcast_fusion = (f32[1,16,512]{2,1,0:T(8,128)}, f32[1,16,512]{2,1,0:T(8,128)}) fusion(f32[32,512]{1,0:T(8,128)S(1)} %shard_map.77), kind=kLoop, calls=%fused_computation.1 | loop fusion | flops 16384 | bytes 131072 | tf_op jit(solution)/shard_map/broadcast_in_dim | solution.py:403

commit v4 on v3

--- a/solution.py
+++ b/solution.py
@@ -19,6 +19,7 @@
 HALVES = 2
 WIDTH = VOX // HALVES
 CHUNKS = 4
+LEVELS = 32767.0
 FAR = 4
 
 
@@ -49,7 +50,10 @@
     rowbuf,
     lhs,
     acc,
+    coded,
     partial,
+    scale,
+    scales,
     over_send,
     over_recv,
     load_sem,
@@ -62,6 +66,8 @@
     data_recv,
     sum_send,
     sum_recv,
+    scale_send,
+    scale_recv,
     over_send_sem,
     over_sem,
 ):
@@ -278,28 +284,58 @@
         def _():
             over_copy(1, half, 1, 0).start()
 
+        sums = acc[half, pl.ds(0, 2 * inner), :].reshape(2 * groups, ROWS_DEV, WIDTH)
+        top = jnp.max(jnp.abs(sums), axis=1, keepdims=True)
+        unit = jnp.where(top > 0.0, LEVELS / jnp.maximum(top, 1e-33), 0.0)
+        code = jnp.round(sums * unit).astype(jnp.int32).astype(jnp.int16)
+        coded[half] = code.reshape(2 * inner, WIDTH)
+        top = top * (1.0 / LEVELS)
+        for g in range(groups):
+            for c in range(2):
+                for n in range(parts):
+                    scale[half, g, pl.ds(c * parts + n, 1), :] = top[
+                        2 * g + c, :, n * PIX : (n + 1) * PIX
+                    ]
+
         for i in range(1, groups):
             peer = frame_peer(i)
             pltpu.make_async_remote_copy(
-                src_ref=acc.at[half, pl.ds(peer * 2 * ROWS_DEV, 2 * ROWS_DEV)],
+                src_ref=scale.at[half, peer],
+                dst_ref=scales.at[half, me_f],
+                send_sem=scale_send.at[half],
+                recv_sem=scale_recv.at[half],
+                device_id={"frame": peer},
+                device_id_type=MESH,
+            ).start()
+            pltpu.make_async_remote_copy(
+                src_ref=coded.at[half, pl.ds(peer * 2 * ROWS_DEV, 2 * ROWS_DEV)],
                 dst_ref=partial.at[half, me_f],
                 send_sem=sum_send.at[half],
                 recv_sem=sum_recv.at[half],
                 device_id={"frame": peer},
                 device_id_type=MESH,
             ).start()
-        partial[half, me_f] = acc[
+        partial[half, me_f] = jnp.zeros((2 * ROWS_DEV, WIDTH), jnp.int16)
+        scales[half, me_f] = jnp.zeros((2 * parts, PIX), jnp.float32)
+        total[:, columns] = acc[
             half, pl.ds(pl.multiple_of(me_f * 2 * ROWS_DEV, 2 * ROWS_DEV), 2 * ROWS_DEV), :
         ]
 
     for half in range(HALVES):
-        columns = pl.ds(half * WIDTH, WIDTH)
         others = partial.at[half, pl.ds(0, groups - 1)]
         pltpu.make_async_copy(others, others, sum_recv.at[half]).wait()
-        value = partial[half, 0]
-        for g in range(1, groups):
-            value = value + partial[half, g]
-        total[:, columns] = value
+        others = scales.at[half, pl.ds(0, groups - 1)]
+        pltpu.make_async_copy(others, others, scale_recv.at[half]).wait()
+        for c in range(2):
+            for n in range(parts):
+                where = (pl.ds(c * ROWS_DEV, ROWS_DEV), pl.ds(half * WIDTH + n * PIX, PIX))
+                value = total[where]
+                for g in range(groups):
+                    term = partial[
+                        half, g, pl.ds(c * ROWS_DEV, ROWS_DEV), pl.ds(n * PIX, PIX)
+                    ]
+                    value = value + term.astype(jnp.float32) * scales[half, g, pl.ds(c * parts + n, 1), :]
+                total[where] = value
 
     def take_overhang(at):
         pltpu.make_async_copy(over_recv, over_recv, over_sem).wait()
@@ -326,6 +362,8 @@
     for half in range(HALVES):
         others = partial.at[half, pl.ds(0, groups - 1)]
         pltpu.make_async_copy(others, others, sum_send.at[half]).wait()
+        others = scales.at[half, pl.ds(0, groups - 1)]
+        pltpu.make_async_copy(others, others, scale_send.at[half]).wait()
 
     def sent_over(side):
         pltpu.make_async_copy(over_send.at[side], over_send.at[side], over_send_sem.at[side]).wait()
@@ -366,7 +404,10 @@
             pltpu.VMEM((2 * SLOTS, PIX), jnp.float32),
             pltpu.VMEM((rows, SLOTS * PIX), jnp.bfloat16),
             pltpu.VMEM((HALVES, rows, WIDTH), jnp.float32),
-            pltpu.VMEM((HALVES, groups, 2 * ROWS_DEV, WIDTH), jnp.float32),
+            pltpu.VMEM((HALVES, 2 * groups * ROWS_DEV, WIDTH), jnp.int16),
+            pltpu.VMEM((HALVES, groups, 2 * ROWS_DEV, WIDTH), jnp.int16),
+            pltpu.VMEM((HALVES, groups, 2 * WIDTH // PIX, PIX), jnp.float32),
+            pltpu.VMEM((HALVES, groups, 2 * WIDTH // PIX, PIX), jnp.float32),
             pltpu.VMEM((2, HALVES, 2 * WIDTH // PIX, PIX), jnp.float32),
             pltpu.VMEM((HALVES, groups, 2 * WIDTH // PIX, PIX), jnp.float32),
             dma((5,)),
@@ -377,6 +418,8 @@
             dma,
             dma,
             dma,
+            dma((HALVES,)),
+            dma((HALVES,)),
             dma((HALVES,)),
             dma((HALVES,)),
             dma((2,)),

time: 31.8 us -> 29.3 us (0.921)
  Pallas kernels: 30.4 us -> 27.8 us
    pallas_call x1, Pallas kernels: 30.4 us -> 27.8 us  [on_device(): pl.pallas_call(functools.partial(kernel, bricks, groups), out_shape=jax.S...]
where the time goes in v4:
time: 29.3 us; the launch traced here: 29 us
  Pallas kernels  27.8 us (95%)
  between operations  0.64 us (2%)
  other arithmetic  0.63 us (2%)
    pallas_call x1, Pallas kernels, on_device(): pl.pallas_call(functools.partial(kernel, bricks, groups), out_shape=jax.S...  27.8 us
    broadcast_in_dim x1, other arithmetic, on_device(): return (merged[None], weight[None])  0.63 us

profile of v4, /device:TPU:1, one launch (start us, length us, event | category | flops | bytes accessed | tf_op | source)
XLA Modules:
  0.0 29.0 jit_solution(12934784992477079262)
XLA Ops:
  0.6 27.8 %shard_map.77 = f32[32,512]{1,0:T(8,128)S(1)} custom-call(s32[4,1,8]{2,1,0:T(1,128)} %pix_hbm.1, s32[4,1,8]{2,1,0:T(1,128)} %vox_hbm.1, s32[4]{0:T(128)} %bitcast.7, f32[4,16,128]{2,1,0:T(8,128)} %intensity_hbm.1, f32[4,16,128]{2,1,0:T(8,128)} %correction_hbm.1, bf16[4096,512]{1,0:T(8,128)(2,1)} %bitcast.6), custom_call_target="tpu_custom_call" | custom-call | tf_op jit(solution)/shard_map/pallas_call | solution.py:388
  28.4 0.6 %slice_bitcast_fusion = (f32[1,16,512]{2,1,0:T(8,128)}, f32[1,16,512]{2,1,0:T(8,128)}) fusion(f32[32,512]{1,0:T(8,128)S(1)} %shard_map.77), kind=kLoop, calls=%fused_computation.1 | loop fusion | flops 16384 | bytes 131072 | tf_op jit(solution)/shard_map/broadcast_in_dim | solution.py:446

commit v5 on v4

--- a/solution.py
+++ b/solution.py
@@ -47,8 +47,8 @@
     request,
     packed,
     received,
-    rowbuf,
     lhs,
+    placer,
     acc,
     coded,
     partial,
@@ -74,10 +74,8 @@
     me_f = lax.axis_index("frame")
     me_b = lax.axis_index("brick")
     near = bricks // FAR
-    me_y = me_b // (2 * FAR)
-    me_c = lax.rem(me_b, 2)
-    me_far = lax.rem(me_b // 2, FAR)
-    me_near = me_y * 2 + me_c
+    me_far = me_b // near
+    me_near = lax.rem(me_b, near)
     held = CAP * FAR
     barrier = pltpu.get_barrier_semaphore()
 
@@ -85,7 +83,9 @@
         return lax.rem(me_b + i, bricks)
 
     def brick_of(at_near, at_far):
-        return (at_near // 2 * FAR + at_far) * 2 + lax.rem(at_near, 2)
+        return at_far * near + at_near
+
+    order = sorted(range(1, near), key=lambda i: (-min(i, near - i), i))
 
     def near_index(i):
         return lax.rem(me_near + i, near)
@@ -99,13 +99,13 @@
     def frame_peer(i):
         return lax.rem(me_f + i, groups)
 
+    for i in order:
+        pl.semaphore_signal(
+            barrier, inc=1, device_id={"brick": near_peer(i)}, device_id_type=MESH
+        )
     for i in range(1, FAR):
         pl.semaphore_signal(
             barrier, inc=1, device_id={"brick": far_peer(i)}, device_id_type=MESH
-        )
-    for i in range(1, near):
-        pl.semaphore_signal(
-            barrier, inc=1, device_id={"brick": near_peer(i)}, device_id_type=MESH
         )
     for i in range(1, groups):
         pl.semaphore_signal(
@@ -143,12 +143,12 @@
     column = jnp.sum(
         jnp.where(sub2 == lane2, jnp.broadcast_to(row, (SLOTS, PIX)), 0), axis=1, keepdims=True
     )
-    near_row = (row // (2 * FAR * PB_DEV)) * 2 + ((row >> 4) & 1)
-    near_col = (column // (2 * FAR * PB_DEV)) * 2 + ((column >> 4) & 1)
+    near_row = (row >> 4) & (near - 1)
+    near_col = (column >> 4) & (near - 1)
     same = (jnp.broadcast_to(near_row, (SLOTS, PIX)) == near_col).astype(jnp.int32)
     rank_row = jnp.sum(jnp.where(sub2 < lane2, same, 0), axis=0, keepdims=True)
     rank_col = jnp.sum(jnp.where(lane2 < sub2, same, 0), axis=1, keepdims=True)
-    where_row = ((row >> 5) & (FAR - 1)) * 128 + (lane >> 3) * PB_DEV + (row & 15)
+    where_row = (row // (near * PB_DEV)) * 128 + (lane >> 3) * PB_DEV + (row & 15)
     code = (near_row * held + rank_row) * 1024 + where_row
     request[me_near] = jnp.where(lane < SLOTS, code, -1)
     key = near_col * held + rank_col
@@ -158,6 +158,25 @@
         axis=0,
     ).astype(jnp.bfloat16)
 
+    inner = groups * ROWS_DEV
+    rows = 2 * inner + 16
+    pieces = 3
+    wide_lane = iota((1, pieces * 2 * SLOTS), 1)
+    voxel = jnp.full((1, pieces * 2 * SLOTS), -1, jnp.int32)
+    for s in range(SLOTS):
+        f, m = s // MAXB, s % MAXB
+        offset = vox_ref[f, 0, m]
+        target = jnp.where(offset == 0, inner, jnp.where(offset == inner + 1, inner + 1, offset - 1))
+        target = jnp.where(m < count_ref[f], target, -1)
+        voxel = jnp.where((wide_lane & (SLOTS - 1)) == s, target, voxel)
+    down = iota((rows, pieces * 2 * SLOTS), 0)
+    tail = down >= 2 * inner
+    own_voxel = jnp.where(tail, inner + (down & 7), (down >> 5) * ROWS_DEV + (down & 15))
+    own_channel = jnp.where(tail, (down >> 3) & 1, (down >> 4) & 1)
+    channel = (iota((rows, pieces * 2 * SLOTS), 1) // SLOTS) & 1
+    hit = (own_voxel == voxel) & (own_channel == channel)
+    placer[...] = jnp.where(hit, 1.0, 0.0).astype(jnp.float32).astype(jnp.bfloat16)
+
     for copy in loads:
         copy.wait()
     pixels[me_far] = jnp.concatenate(
@@ -167,6 +186,15 @@
 
     pl.semaphore_wait(barrier, FAR - 1 + near - 1 + groups - 1)
 
+    for i in order:
+        pltpu.make_async_remote_copy(
+            src_ref=request.at[me_near],
+            dst_ref=request.at[me_near],
+            send_sem=req_send,
+            recv_sem=req_recv,
+            device_id={"brick": near_peer(i)},
+            device_id_type=MESH,
+        ).start()
     for i in range(1, FAR):
         pltpu.make_async_remote_copy(
             src_ref=pixels.at[me_far],
@@ -176,15 +204,6 @@
             device_id={"brick": far_peer(i)},
             device_id_type=MESH,
         ).start()
-    for i in range(1, near):
-        pltpu.make_async_remote_copy(
-            src_ref=request.at[me_near],
-            dst_ref=request.at[me_near],
-            send_sem=req_send,
-            recv_sem=req_recv,
-            device_id={"brick": near_peer(i)},
-            device_id_type=MESH,
-        ).start()
 
     def others_of(buffer, count, sem):
         others = buffer.at[pl.ds(0, count - 1)]
@@ -208,7 +227,7 @@
     ).astype(jnp.bfloat16)
     packed[...] = blocks.reshape(near, 2 * held, PIX)
 
-    for i in range(1, near):
+    for i in order:
         pltpu.make_async_remote_copy(
             src_ref=packed.at[near_index(i)],
             dst_ref=received.at[me_near],
@@ -220,37 +239,12 @@
     received[me_near] = packed[me_near]
     others_of(received, near, data_recv).wait()
 
-    rowbuf[...] = jnp.dot(
+    rows_of = jnp.dot(
         pick, received[...].reshape(near * 2 * held, PIX), preferred_element_type=jnp.float32
     )
-
-    inner = groups * ROWS_DEV
-
-    def place_slot(f, m, carry):
-        s = f * MAXB + m
-        offset = vox_ref[f, 0, m]
-        target = jnp.where(offset == 0, inner, jnp.where(offset == inner + 1, inner + 1, offset - 1))
-        target = jnp.where(m < count_ref[f], target, -1)
-        hit = iota((inner + 8, PIX), 0) == target
-        start = pl.multiple_of(s * PIX, PIX)
-        parts = []
-        for c in range(2):
-            value = jnp.broadcast_to(rowbuf[pl.ds(c * SLOTS + s, 1), :], (inner + 8, PIX))
-            parts.append(jnp.where(hit, value, 0.0))
-        for g in range(groups):
-            for c in range(2):
-                lhs[pl.ds((2 * g + c) * ROWS_DEV, ROWS_DEV), pl.ds(start, PIX)] = parts[c][
-                    g * ROWS_DEV : (g + 1) * ROWS_DEV
-                ].astype(jnp.bfloat16)
-        lhs[pl.ds(2 * inner, 16), pl.ds(start, PIX)] = jnp.concatenate(
-            [part[inner:] for part in parts], axis=0
-        ).astype(jnp.bfloat16)
-        return carry
-
-    def place_frame(f, carry):
-        return lax.fori_loop(0, MAXB, functools.partial(place_slot, f), carry)
-
-    lax.fori_loop(0, FR_DEV, place_frame, 0)
+    slot = iota((2 * SLOTS, PIX), 0) & (SLOTS - 1)
+    for s in range(SLOTS):
+        lhs[:, s * PIX : (s + 1) * PIX] = jnp.where(slot == s, rows_of, 0.0).astype(jnp.bfloat16)
     for copy in splits:
         copy.wait()
 
@@ -267,7 +261,16 @@
     parts = WIDTH // PIX
     for half in range(HALVES):
         columns = pl.ds(half * WIDTH, WIDTH)
-        acc[half] = jnp.dot(lhs[...], split[:, columns], preferred_element_type=jnp.float32)
+        contrib = jnp.dot(lhs[...], split[:, columns], preferred_element_type=jnp.float32)
+        first = contrib.astype(jnp.bfloat16)
+        left = contrib - first.astype(jnp.float32)
+        second = left.astype(jnp.bfloat16)
+        third = (left - second.astype(jnp.float32)).astype(jnp.bfloat16)
+        acc[half] = jnp.dot(
+            placer[...],
+            jnp.concatenate([first, second, third], axis=0),
+            preferred_element_type=jnp.float32,
+        )
 
         for side in range(2):
             for c in range(2):
@@ -401,8 +404,8 @@
             pltpu.VMEM((near, 1, PIX), jnp.int32),
             pltpu.VMEM((near, message, PIX), jnp.bfloat16),
             pltpu.VMEM((near, message, PIX), jnp.bfloat16),
-            pltpu.VMEM((2 * SLOTS, PIX), jnp.float32),
-            pltpu.VMEM((rows, SLOTS * PIX), jnp.bfloat16),
+            pltpu.VMEM((2 * SLOTS, SLOTS * PIX), jnp.bfloat16),
+            pltpu.VMEM((rows, 6 * SLOTS), jnp.bfloat16),
             pltpu.VMEM((HALVES, rows, WIDTH), jnp.float32),
             pltpu.VMEM((HALVES, 2 * groups * ROWS_DEV, WIDTH), jnp.int16),
             pltpu.VMEM((HALVES, groups, 2 * ROWS_DEV, WIDTH), jnp.int16),

time: 29.3 us -> 28.1 us (0.959)
  Pallas kernels: 27.8 us -> 26.7 us
    pallas_call x1, Pallas kernels: 27.8 us -> 26.7 us  [on_device(): pl.pallas_call(functools.partial(kernel, bricks, groups), out_shape=jax.S...]
where the time goes in v5:
time: 28.1 us; the launch traced here: 28 us
  Pallas kernels  26.7 us (95%)
  between operations  0.64 us (2%)
  other arithmetic  0.63 us (2%)
    pallas_call x1, Pallas kernels, on_device(): pl.pallas_call(functools.partial(kernel, bricks, groups), out_shape=jax.S...  26.7 us
    broadcast_in_dim x1, other arithmetic, on_device(): return (merged[None], weight[None])  0.63 us

profile of v5, /device:TPU:1, one launch (start us, length us, event | category | flops | bytes accessed | tf_op | source)
XLA Modules:
  0.0 28.0 jit_solution(12467607450213270360)
XLA Ops:
  0.6 26.7 %shard_map.77 = f32[32,512]{1,0:T(8,128)S(1)} custom-call(s32[4,1,8]{2,1,0:T(1,128)} %pix_hbm.1, s32[4,1,8]{2,1,0:T(1,128)} %vox_hbm.1, s32[4]{0:T(128)} %bitcast.7, f32[4,16,128]{2,1,0:T(8,128)} %intensity_hbm.1, f32[4,16,128]{2,1,0:T(8,128)} %correction_hbm.1, bf16[4096,512]{1,0:T(8,128)(2,1)} %bitcast.6), custom_call_target="tpu_custom_call" | custom-call | tf_op jit(solution)/shard_map/pallas_call | solution.py:391
  27.4 0.6 %slice_bitcast_fusion = (f32[1,16,512]{2,1,0:T(8,128)}, f32[1,16,512]{2,1,0:T(8,128)}) fusion(f32[32,512]{1,0:T(8,128)S(1)} %shard_map.77), kind=kLoop, calls=%fused_computation.1 | loop fusion | flops 16384 | bytes 131072 | tf_op jit(solution)/shard_map/broadcast_in_dim | solution.py:449

commit v6 on v5

--- a/solution.py
+++ b/solution.py
@@ -16,7 +16,7 @@
 SLOTS = FR_DEV * MAXB
 PIX = 128
 VOX = 512
-HALVES = 2
+HALVES = 1
 WIDTH = VOX // HALVES
 CHUNKS = 4
 LEVELS = 32767.0

time: 28.1 us -> 27.3 us (0.972)
  Pallas kernels: 26.7 us -> 25.9 us
    pallas_call x1, Pallas kernels: 26.7 us -> 25.9 us  [on_device(): pl.pallas_call(functools.partial(kernel, bricks, groups), out_shape=jax.S...]
where the time goes in v6:
time: 27.3 us; the launch traced here: 27.1 us
  Pallas kernels  25.9 us (95%)
  between operations  0.64 us (2%)
  other arithmetic  0.63 us (2%)
    pallas_call x1, Pallas kernels, on_device(): pl.pallas_call(functools.partial(kernel, bricks, groups), out_shape=jax.S...  25.9 us
    broadcast_in_dim x1, other arithmetic, on_device(): return (merged[None], weight[None])  0.63 us

profile of v6, /device:TPU:1, one launch (start us, length us, event | category | flops | bytes accessed | tf_op | source)
XLA Modules:
  0.0 27.1 jit_solution(8380732720861320083)
XLA Ops:
  0.6 25.9 %shard_map.77 = f32[32,512]{1,0:T(8,128)S(1)} custom-call(s32[4,1,8]{2,1,0:T(1,128)} %pix_hbm.1, s32[4,1,8]{2,1,0:T(1,128)} %vox_hbm.1, s32[4]{0:T(128)} %bitcast.7, f32[4,16,128]{2,1,0:T(8,128)} %intensity_hbm.1, f32[4,16,128]{2,1,0:T(8,128)} %correction_hbm.1, bf16[4096,512]{1,0:T(8,128)(2,1)} %bitcast.6), custom_call_target="tpu_custom_call" | custom-call | tf_op jit(solution)/shard_map/pallas_call | solution.py:391
  26.5 0.6 %slice_bitcast_fusion = (f32[1,16,512]{2,1,0:T(8,128)}, f32[1,16,512]{2,1,0:T(8,128)}) fusion(f32[32,512]{1,0:T(8,128)S(1)} %shard_map.77), kind=kLoop, calls=%fused_computation.1 | loop fusion | flops 16384 | bytes 131072 | tf_op jit(solution)/shard_map/broadcast_in_dim | solution.py:449

commit v7 on v6

--- a/solution.py
+++ b/solution.py
@@ -60,6 +60,7 @@
     split_sem,
     pix_send,
     pix_recv,
+    met,
     req_send,
     req_recv,
     data_send,
@@ -74,8 +75,10 @@
     me_f = lax.axis_index("frame")
     me_b = lax.axis_index("brick")
     near = bricks // FAR
-    me_far = me_b // near
-    me_near = lax.rem(me_b, near)
+    me_y = me_b // (2 * FAR)
+    me_c = lax.rem(me_b, 2)
+    me_far = lax.rem(me_b // 2, FAR)
+    me_near = me_y * 2 + me_c
     held = CAP * FAR
     barrier = pltpu.get_barrier_semaphore()
 
@@ -83,7 +86,7 @@
         return lax.rem(me_b + i, bricks)
 
     def brick_of(at_near, at_far):
-        return at_far * near + at_near
+        return (at_near // 2 * FAR + at_far) * 2 + lax.rem(at_near, 2)
 
     order = sorted(range(1, near), key=lambda i: (-min(i, near - i), i))
 
@@ -96,21 +99,42 @@
     def far_peer(i):
         return brick_of(me_near, lax.rem(me_far + i, FAR))
 
+    line = groups // 2
+    me_line = me_f // line
+    other_core = me_b + 1 - 2 * lax.rem(me_b, 2)
+
+    def line_peer(i):
+        return me_line * line + lax.rem(me_f + i, line)
+
     def frame_peer(i):
         return lax.rem(me_f + i, groups)
 
-    for i in order:
-        pl.semaphore_signal(
-            barrier, inc=1, device_id={"brick": near_peer(i)}, device_id_type=MESH
-        )
     for i in range(1, FAR):
         pl.semaphore_signal(
             barrier, inc=1, device_id={"brick": far_peer(i)}, device_id_type=MESH
         )
-    for i in range(1, groups):
+    for i in range(2, near, 2):
         pl.semaphore_signal(
-            barrier, inc=1, device_id={"frame": frame_peer(i)}, device_id_type=MESH
+            barrier, inc=1, device_id={"brick": near_peer(i)}, device_id_type=MESH
         )
+    pl.semaphore_signal(barrier, inc=1, device_id={"brick": other_core}, device_id_type=MESH)
+    for i in range(1, line):
+        pl.semaphore_signal(
+            barrier, inc=1, device_id={"frame": line_peer(i)}, device_id_type=MESH
+        )
+    pl.semaphore_signal(
+        barrier, inc=1, device_id={"frame": frame_peer(line)}, device_id_type=MESH
+    )
+
+    @pl.when((me_f == 0) | (me_f == groups - 1))
+    def _():
+        for i in range(1, line):
+            pl.semaphore_signal(
+                barrier,
+                inc=1,
+                device_id={"frame": (1 - me_line) * line + lax.rem(me_f + i, line)},
+                device_id_type=MESH,
+            )
 
     tables = [
         pltpu.make_async_copy(pix_hbm, pix_ref, load_sem.at[0]),
@@ -143,12 +167,12 @@
     column = jnp.sum(
         jnp.where(sub2 == lane2, jnp.broadcast_to(row, (SLOTS, PIX)), 0), axis=1, keepdims=True
     )
-    near_row = (row >> 4) & (near - 1)
-    near_col = (column >> 4) & (near - 1)
+    near_row = (row // (2 * FAR * PB_DEV)) * 2 + ((row >> 4) & 1)
+    near_col = (column // (2 * FAR * PB_DEV)) * 2 + ((column >> 4) & 1)
     same = (jnp.broadcast_to(near_row, (SLOTS, PIX)) == near_col).astype(jnp.int32)
     rank_row = jnp.sum(jnp.where(sub2 < lane2, same, 0), axis=0, keepdims=True)
     rank_col = jnp.sum(jnp.where(lane2 < sub2, same, 0), axis=1, keepdims=True)
-    where_row = (row // (near * PB_DEV)) * 128 + (lane >> 3) * PB_DEV + (row & 15)
+    where_row = ((row >> 5) & (FAR - 1)) * 128 + (lane >> 3) * PB_DEV + (row & 15)
     code = (near_row * held + rank_row) * 1024 + where_row
     request[me_near] = jnp.where(lane < SLOTS, code, -1)
     key = near_col * held + rank_col
@@ -184,8 +208,37 @@
         axis=0,
     ).astype(jnp.bfloat16)
 
-    pl.semaphore_wait(barrier, FAR - 1 + near - 1 + groups - 1)
-
+    ends = jnp.where((me_f == line - 1) | (me_f == line), 0, 1)
+    pl.semaphore_wait(barrier, FAR - 1 + near // 2 - 1 + 1 + line - 1 + 1 + ends)
+    pl.semaphore_signal(met.at[0], inc=1, device_id={"brick": other_core}, device_id_type=MESH)
+    pl.semaphore_signal(
+        met.at[1], inc=1, device_id={"frame": frame_peer(line)}, device_id_type=MESH
+    )
+
+    def push(i):
+        pltpu.make_async_remote_copy(
+            src_ref=pixels.at[me_far],
+            dst_ref=pixels.at[me_far],
+            send_sem=pix_send,
+            recv_sem=pix_recv,
+            device_id={"brick": far_peer(i)},
+            device_id_type=MESH,
+        ).start()
+
+    for i in range(FAR - 1, 0, -1):
+
+        @pl.when(me_far >= i)
+        def _():
+            push(FAR - i)
+
+    for i in range(FAR - 1, 0, -1):
+
+        @pl.when(me_far + i < FAR)
+        def _():
+            push(i)
+
+    pl.semaphore_wait(met.at[0], 1)
+    pl.semaphore_wait(met.at[1], 1)
     for i in order:
         pltpu.make_async_remote_copy(
             src_ref=request.at[me_near],
@@ -193,15 +246,6 @@
             send_sem=req_send,
             recv_sem=req_recv,
             device_id={"brick": near_peer(i)},
-            device_id_type=MESH,
-        ).start()
-    for i in range(1, FAR):
-        pltpu.make_async_remote_copy(
-            src_ref=pixels.at[me_far],
-            dst_ref=pixels.at[me_far],
-            send_sem=pix_send,
-            recv_sem=pix_recv,
-            device_id={"brick": far_peer(i)},
             device_id_type=MESH,
         ).start()
 
@@ -417,6 +461,7 @@
             dma((CHUNKS,)),
             dma,
             dma,
+            pltpu.SemaphoreType.REGULAR((2,)),
             dma,
             dma,
             dma,

time: 27.3 us -> 27 us (0.989)
  Pallas kernels: 25.9 us -> 25.5 us
    pallas_call x1, Pallas kernels: 25.9 us -> 25.5 us  [on_device(): pl.pallas_call(functools.partial(kernel, bricks, groups), out_shape=jax.S...]
where the time goes in v7:
time: 27 us; the launch traced here: 26.8 us
  Pallas kernels  25.5 us (94%)
  between operations  0.64 us (2%)
  other arithmetic  0.63 us (2%)
    pallas_call x1, Pallas kernels, on_device(): pl.pallas_call(functools.partial(kernel, bricks, groups), out_shape=jax.S...  25.5 us
    broadcast_in_dim x1, other arithmetic, on_device(): return (merged[None], weight[None])  0.63 us

profile of v7, /device:TPU:1, one launch (start us, length us, event | category | flops | bytes accessed | tf_op | source)
XLA Modules:
  0.0 26.8 jit_solution(14028720915365771466)
XLA Ops:
  0.6 25.5 %shard_map.77 = f32[32,512]{1,0:T(8,128)S(1)} custom-call(s32[4,1,8]{2,1,0:T(1,128)} %pix_hbm.1, s32[4,1,8]{2,1,0:T(1,128)} %vox_hbm.1, s32[4]{0:T(128)} %bitcast.7, f32[4,16,128]{2,1,0:T(8,128)} %intensity_hbm.1, f32[4,16,128]{2,1,0:T(8,128)} %correction_hbm.1, bf16[4096,512]{1,0:T(8,128)(2,1)} %bitcast.6), custom_call_target="tpu_custom_call" | custom-call | tf_op jit(solution)/shard_map/pallas_call | solution.py:435
  26.2 0.6 %slice_bitcast_fusion = (f32[1,16,512]{2,1,0:T(8,128)}, f32[1,16,512]{2,1,0:T(8,128)}) fusion(f32[32,512]{1,0:T(8,128)S(1)} %shard_map.77), kind=kLoop, calls=%fused_computation.1 | loop fusion | flops 16384 | bytes 131072 | tf_op jit(solution)/shard_map/broadcast_in_dim | solution.py:494

commit v8 on v7

--- a/solution.py
+++ b/solution.py
@@ -332,9 +332,8 @@
             over_copy(1, half, 1, 0).start()
 
         sums = acc[half, pl.ds(0, 2 * inner), :].reshape(2 * groups, ROWS_DEV, WIDTH)
-        top = jnp.max(jnp.abs(sums), axis=1, keepdims=True)
-        unit = jnp.where(top > 0.0, LEVELS / jnp.maximum(top, 1e-33), 0.0)
-        code = jnp.round(sums * unit).astype(jnp.int32).astype(jnp.int16)
+        top = jnp.maximum(jnp.max(jnp.abs(sums), axis=1, keepdims=True), 1e-33)
+        code = jnp.round(sums * (LEVELS / top)).astype(jnp.int32).astype(jnp.int16)
         coded[half] = code.reshape(2 * inner, WIDTH)
         top = top * (1.0 / LEVELS)
         for g in range(groups):

time: 27 us -> 26.9 us (level)
  no operation moved by 1% of the time
where the time goes in v8:
time: 26.9 us; the launch traced here: 26.8 us
  Pallas kernels  25.5 us (95%)
  between operations  0.64 us (2%)
  other arithmetic  0.63 us (2%)
    pallas_call x1, Pallas kernels, on_device(): pl.pallas_call(functools.partial(kernel, bricks, groups), out_shape=jax.S...  25.5 us
    broadcast_in_dim x1, other arithmetic, on_device(): return (merged[None], weight[None])  0.63 us

profile of v8, /device:TPU:1, one launch (start us, length us, event | category | flops | bytes accessed | tf_op | source)
XLA Modules:
  0.0 26.8 jit_solution(9888587515311694742)
XLA Ops:
  0.6 25.5 %shard_map.77 = f32[32,512]{1,0:T(8,128)S(1)} custom-call(s32[4,1,8]{2,1,0:T(1,128)} %pix_hbm.1, s32[4,1,8]{2,1,0:T(1,128)} %vox_hbm.1, s32[4]{0:T(128)} %bitcast.7, f32[4,16,128]{2,1,0:T(8,128)} %intensity_hbm.1, f32[4,16,128]{2,1,0:T(8,128)} %correction_hbm.1, bf16[4096,512]{1,0:T(8,128)(2,1)} %bitcast.6), custom_call_target="tpu_custom_call" | custom-call | tf_op jit(solution)/shard_map/pallas_call | solution.py:434
  26.2 0.6 %slice_bitcast_fusion = (f32[1,16,512]{2,1,0:T(8,128)}, f32[1,16,512]{2,1,0:T(8,128)}) fusion(f32[32,512]{1,0:T(8,128)S(1)} %shard_map.77), kind=kLoop, calls=%fused_computation.1 | loop fusion | flops 16384 | bytes 131072 | tf_op jit(solution)/shard_map/broadcast_in_dim | solution.py:493

commit v9 on v8

--- a/solution.py
+++ b/solution.py
@@ -285,10 +285,10 @@
 
     rows_of = jnp.dot(
         pick, received[...].reshape(near * 2 * held, PIX), preferred_element_type=jnp.float32
-    )
+    ).astype(jnp.bfloat16)
     slot = iota((2 * SLOTS, PIX), 0) & (SLOTS - 1)
     for s in range(SLOTS):
-        lhs[:, s * PIX : (s + 1) * PIX] = jnp.where(slot == s, rows_of, 0.0).astype(jnp.bfloat16)
+        lhs[:, s * PIX : (s + 1) * PIX] = jnp.where(slot == s, rows_of, jnp.bfloat16(0.0))
     for copy in splits:
         copy.wait()
 

time: 26.9 us -> 27 us (level)
  no operation moved by 1% of the time
where the time goes in v9:
time: 27 us; the launch traced here: 26.8 us
  Pallas kernels  25.5 us (94%)
  between operations  0.64 us (2%)
  other arithmetic  0.63 us (2%)
    pallas_call x1, Pallas kernels, on_device(): pl.pallas_call(functools.partial(kernel, bricks, groups), out_shape=jax.S...  25.5 us
    broadcast_in_dim x1, other arithmetic, on_device(): return (merged[None], weight[None])  0.63 us

profile of v9, /device:TPU:1, one launch (start us, length us, event | category | flops | bytes accessed | tf_op | source)
XLA Modules:
  0.0 26.8 jit_solution(17706539568874817928)
XLA Ops:
  0.6 25.5 %shard_map.77 = f32[32,512]{1,0:T(8,128)S(1)} custom-call(s32[4,1,8]{2,1,0:T(1,128)} %pix_hbm.1, s32[4,1,8]{2,1,0:T(1,128)} %vox_hbm.1, s32[4]{0:T(128)} %bitcast.7, f32[4,16,128]{2,1,0:T(8,128)} %intensity_hbm.1, f32[4,16,128]{2,1,0:T(8,128)} %correction_hbm.1, bf16[4096,512]{1,0:T(8,128)(2,1)} %bitcast.6), custom_call_target="tpu_custom_call" | custom-call | tf_op jit(solution)/shard_map/pallas_call | solution.py:434
  26.2 0.6 %slice_bitcast_fusion = (f32[1,16,512]{2,1,0:T(8,128)}, f32[1,16,512]{2,1,0:T(8,128)}) fusion(f32[32,512]{1,0:T(8,128)S(1)} %shard_map.77), kind=kLoop, calls=%fused_computation.1 | loop fusion | flops 16384 | bytes 131072 | tf_op jit(solution)/shard_map/broadcast_in_dim | solution.py:493
